TPU v7x, 32 devices: a whole 2x2x4 slice. The times are simulated.
32 devices in a mesh: rows: 8 (over y, x, core), sub: 4 (over z).
Axes of the slice: x: 2, y: 2, z: 4, core: 2. Of those that a mesh axis runs over, the one named last changes fastest.
Arguments:
- old_basis: bfloat16 [32, 524288], P(None, ('rows', 'sub')), may hold values from -1 to 1
- snapshots: bfloat16 [512, 524288], P(None, ('rows', 'sub')), may hold values from -16 to 16
- gap_flags: int32 [512, 4096], P(None, ('rows', 'sub')), may hold values from 0 to 1, as said below
- sketch_seed: int32 [512, 64], replicated, may hold values from -1 to 1
Outputs:
- new_basis: float32 [32, 524288], P(None, ('rows', 'sub'))
- coefficients: float32 [32, 512], replicated
Inputs may be any that keep to these rules, and one draw needn't show every extreme that they name: `gap_flags`: 1 marks a block of 128 velocity rows measured in that snapshot, 0 a gap; every snapshot has measured blocks and gaps.
All inputs are finite; a program needn't handle non-finite values.
Results may differ from a plain program's by a relative error of at most 0.00135.
The roundings to bfloat16 on the way count: a program that leaves them out, or rounds other values in their place, can miss the bound.
Values may be sent and summed in bfloat16 or wider, within the bound.
No kernel may reach another device: no remote copies, remote signals or barrier semaphores. Data moves between devices by JAX's collectives and lax.ppermute only.
A program may use at most 192 MiB of HBM per device.

v0:
```python
import math
import jax
import jax.numpy as jnp
from jax import lax
from jax.sharding import PartitionSpec as P

POWER = 2
damping = 0.005
highest = lax.Precision.HIGHEST


def cholesky_last(system):
    extent = system.shape[0]
    factor = jnp.zeros_like(system)
    for column in range(extent):
        partial_sum = jnp.sum(factor * factor[column : column + 1], axis=1)
        remain = system[:, column] - partial_sum
        diagonal_root = jnp.sqrt(remain[column])
        lower_part = (jnp.arange(extent) >= column).reshape((extent,) + (1,) * (system.ndim - 2))
        factor = factor.at[:, column].set(jnp.where(lower_part, remain / diagonal_root, 0.0))
    return factor


def lower_solve(factor, target):
    extent = factor.shape[0]
    result = jnp.zeros_like(target)
    for column in range(extent):
        current = (target[column] - jnp.sum(factor[column] * result, axis=0)) / factor[
            column, column
        ]
        result = result.at[column].set(current)
    return result


def upper_solve(factor, target):
    extent = factor.shape[0]
    result = jnp.zeros_like(target)
    for column in reversed(range(extent)):
        current = (target[column] - jnp.sum(factor[:, column] * result, axis=0)) / factor[
            column, column
        ]
        result = result.at[column].set(current)
    return result


def solve_normal(grams, right, modes, rows_all):
    snapshot_count = grams.shape[0]
    identity = jnp.eye(modes, dtype=jnp.float32)[:, :, None]
    system = grams.T.reshape(modes, modes, snapshot_count) + damping * rows_all * identity
    factor = cholesky_last(system)
    return upper_solve(factor, lower_solve(factor, right.T))


def inverse_factor(products):
    extent = products.shape[0]
    factor = cholesky_last(products[:, :, None])
    return lower_solve(factor, jnp.eye(extent, dtype=jnp.float32))


def mask_blocks(samples, flag_blocks):
    snapshot_count, blocks_dev = flag_blocks.shape
    weights = flag_blocks.astype(samples.dtype)[:, :, None]
    return (samples.reshape(snapshot_count, blocks_dev, -1) * weights).reshape(snapshot_count, -1)


def refill(samples, flag_blocks, recon_low):
    snapshot_count, blocks_dev = flag_blocks.shape
    observed = (flag_blocks > 0)[:, :, None]
    combined = jnp.where(
        observed,
        samples.reshape(snapshot_count, blocks_dev, -1),
        recon_low.reshape(snapshot_count, blocks_dev, -1),
    )
    return combined.reshape(snapshot_count, -1)


def contract_rows(former, latter):
    return lax.dot_general(
        former, latter, (((1,), (1,)), ((), ())), preferred_element_type=jnp.float32
    )


def contract_first(former, latter):
    return lax.dot_general(
        former, latter, (((0,), (0,)), ((), ())), preferred_element_type=jnp.float32
    )


def per_device(old_basis, snapshots, gap_flags, sketch_seed):
    modes = old_basis.shape[0]
    rows_all = old_basis.shape[1] * lax.axis_size(("rows", "sub"))
    blocks_dev = gap_flags.shape[1]
    masked = mask_blocks(snapshots, gap_flags)
    right = contract_rows(masked, old_basis)
    pieces = old_basis.reshape(modes, blocks_dev, -1)
    block_grams = jnp.einsum("kbi,lbi->bkl", pieces, pieces, preferred_element_type=jnp.float32)
    block_rows = block_grams.reshape(blocks_dev, modes * modes)
    grams = jnp.dot(gap_flags.astype(jnp.float32), block_rows, precision=highest)
    mixer = sketch_seed.astype(jnp.bfloat16)
    gram_total, right_total = lax.psum((grams, right), ("rows", "sub"))
    coefficients = solve_normal(gram_total, right_total, modes, rows_all)
    recon_low = contract_first(coefficients.astype(jnp.bfloat16), old_basis).astype(jnp.bfloat16)
    filled = refill(snapshots, gap_flags, recon_low)
    sketch = contract_first(mixer, filled)
    inverse = None
    for sweep_index in range(POWER + 1):
        if sweep_index > 0:
            sketch = contract_first(mixer, filled)
        local_gram = lax.dot_general(
            sketch,
            sketch,
            (((1,), (1,)), ((), ())),
            precision=highest,
            preferred_element_type=jnp.float32,
        )
        products = lax.psum(local_gram, ("rows", "sub"))
        inverse = inverse_factor(products)
        if sweep_index < POWER:
            ortho_rows = jnp.dot(inverse, sketch, precision=highest).astype(jnp.bfloat16)
            mixer_share = lax.psum_scatter(
                contract_rows(filled, ortho_rows), ("rows", "sub"), scatter_dimension=0, tiled=True
            ).astype(jnp.bfloat16)
            mixer = lax.all_gather(mixer_share, ("rows", "sub"), axis=0, tiled=True)
    root_rows = math.sqrt(rows_all)
    new_basis = jnp.dot(inverse[:modes], sketch, precision=highest) * root_rows
    return (new_basis, coefficients)


def solution(mesh):
    in_specs = (P(None, ("rows", "sub")), P(None, ("rows", "sub")), P(None, ("rows", "sub")), P())
    out_specs = (P(None, ("rows", "sub")), P())
    return jax.shard_map(
        per_device, mesh=mesh, in_specs=in_specs, out_specs=out_specs, check_vma=False
    )
```

profile of v0, /device:TPU:0, one launch (start us, length us, event | category | flops | bytes accessed | tf_op | source)
XLA Modules:
  0.0 1549.7 jit_solution(17264317991794373059)
XLA Ops:
  9.1 2.1 copy.518
  11.2 2.8 fusion.6
  14.1 2.5 copy.519
  16.6 13.0 mul.4308
  29.6 24.4 %fusion.2 = f32[32,512]{1,0:T(8,128)} fusion(bf16[32,16384]{1,0:T(8,128)(2,1)S(1)} %copy-done, bf16[512,16384]{1,0:T(8,128)(2,1)} %param.965, bf16[64,8,128,128]{3,2,1,0:T(8,128)(2,1)} %bitcast.3922), kind=kOutput, calls=%fused_computation.40 | convolution fusion | flops 545259520 | bytes 34668544 | tf_op jit(solution)/shard_map/dot_general | solution.py:78
  54.7 137.0 %all-reduce.12.cloned.1.call-done = (f32[32,32,512]{2,0,1:T(8,128)}, f32[32,512]{1,0:T(8,128)}) async-done(((f32[32,32,512]{2,0,1:T(8,128)}, f32[32,512]{1,0:T(8,128)}), (f32[32,32,512]{2,0,1:T(8,128)}, f32[32,512]{1,0:T(8,128)})) %all-reduce.12.cloned.1.call-update) | async-done | bytes 2162704 | tf_op jit(solution)/shard_map/psum | solution.py:100
  191.7 1.8 broadcast_add_fusion
  291.6 12.0 broadcast_in_dim.635
  303.5 15.2 bitcast_select_fusion
  318.8 8.8 fusion.224
  327.6 1.9 copy-done.5
  329.5 3.4 convolution_bitcast_fusion.2
  332.9 39.6 %psum.37 = f32[64,64,1]{1,0,2:T(8,128)S(1)} all-reduce(f32[64,64,1]{1,0,2:T(8,128)S(1)} %convolution_bitcast_fusion.2), channel_id=1, replica_groups=mesh['rows'=8,'sub'=4] {'rows','sub'}, use_global_device_ids=true, to_apply=%region_97.98 | all-reduce | flops 4096 | bytes 32768 | tf_op jit(solution)/shard_map/psum | solution.py:116
  498.8 1.4 fusion.505
  500.2 1.4 fusion.504
  510.2 1.4 fusion.497
  511.7 1.4 fusion.496
  516.1 1.4 fusion.493
  530.4 1.4 fusion.483
  537.6 1.4 fusion.478
  566.0 1.4 fusion.458
  578.8 1.4 fusion.449
  581.6 6.0 convolution_convert_fusion.2
  587.6 8.8 fusion.526
  596.5 133.4 %reduce-scatter.3.cloned.1.call-done = f32[16,64]{1,0:T(8,128)} async-done(((f32[512,64]{1,0:T(8,128)}), f32[16,64]{1,0:T(8,128)}) %reduce-scatter.3.cloned.1.call-update) | async-done | bytes 4112 | tf_op jit(solution)/shard_map/reduce_scatter | solution.py:120
  730.6 64.8 %all_gather.6 = bf16[512,64]{1,0:T(8,128)(2,1)S(1)} all-gather(bf16[16,64]{1,0:T(8,128)(2,1)S(1)} %convert_element_type.415), channel_id=1, replica_groups=mesh['rows'=8,'sub'=4] {'rows','sub'}, dimensions={0}, use_global_device_ids=true | all-gather | bytes 67584 | tf_op jit(solution)/shard_map/all_gather | solution.py:123
  795.3 8.9 fusion.527
  804.2 1.9 copy-done.4
  806.2 3.4 convolution_bitcast_fusion.1
  809.6 39.9 %psum.38 = f32[64,64,1]{1,0,2:T(8,128)S(1)} all-reduce(f32[64,64,1]{1,0,2:T(8,128)S(1)} %convolution_bitcast_fusion.1), channel_id=1, replica_groups=mesh['rows'=8,'sub'=4] {'rows','sub'}, use_global_device_ids=true, to_apply=%region_226.227 | all-reduce | flops 4096 | bytes 32768 | tf_op jit(solution)/shard_map/psum | solution.py:116
  970.7 1.9 subtract_divide_fusion.3
  972.7 1.4 fusion.447
  974.2 1.4 fusion.446
  979.9 1.4 fusion.442
  981.4 1.4 fusion.441
  991.3 1.4 fusion.434
  997.2 1.4 fusion.430
  1011.5 1.4 fusion.420
  1018.7 1.4 fusion.415
  1047.1 1.4 fusion.395
  1059.9 1.4 fusion.386
  1062.7 6.0 convolution_convert_fusion.1
  1068.7 8.8 fusion.528
  1077.5 133.0 %reduce-scatter.5.cloned.1.call-done = f32[16,64]{1,0:T(8,128)} async-done(((f32[512,64]{1,0:T(8,128)}), f32[16,64]{1,0:T(8,128)}) %reduce-scatter.5.cloned.1.call-update) | async-done | bytes 4112 | tf_op jit(solution)/shard_map/reduce_scatter | solution.py:120
  1211.2 64.8 %all_gather.7 = bf16[512,64]{1,0:T(8,128)(2,1)S(1)} all-gather(bf16[16,64]{1,0:T(8,128)(2,1)S(1)} %convert_element_type.417), channel_id=1, replica_groups=mesh['rows'=8,'sub'=4] {'rows','sub'}, dimensions={0}, use_global_device_ids=true | all-gather | bytes 67584 | tf_op jit(solution)/shard_map/all_gather | solution.py:123
  1276.0 8.9 fusion.529
  1284.9 1.9 copy-done.3
  1286.8 3.4 convolution_bitcast_fusion
  1290.2 39.9 %psum.39 = f32[64,64,1]{1,0,2:T(8,128)S(1)} all-reduce(f32[64,64,1]{1,0,2:T(8,128)S(1)} %convolution_bitcast_fusion), channel_id=1, replica_groups=mesh['rows'=8,'sub'=4] {'rows','sub'}, use_global_device_ids=true, to_apply=%region_355.356 | all-reduce | flops 4096 | bytes 32768 | tf_op jit(solution)/shard_map/psum | solution.py:116
  1450.6 1.9 subtract_divide_fusion.2
  1452.6 1.4 fusion.384
  1455.5 1.4 fusion.382
  1462.7 1.4 fusion.377
  1467.0 1.4 fusion.374
  1468.5 1.4 fusion.373
  1471.4 1.4 fusion.371
  1482.8 1.4 fusion.363
  1484.2 1.4 fusion.362
  1498.5 1.4 fusion.352
  1508.6 1.4 fusion.345
  1520.1 1.4 fusion.337
  1530.0 1.4 fusion.330
  1532.9 1.4 fusion.328
  1537.1 5.7 convolution_multiply_fusion
  (2302 shorter events, 543.1 us)
Async XLA Ops:
  7.2 1.3 copy-start
  7.2 184.5 %all-reduce.12.cloned.1.call-start = ((), (), s32[]{:S(2)}) async-start(), calls=%async_computation.4 | async-start | bytes 4325376 | tf_op jit(solution)/shard_map/psum | solution.py:100
  9.1 2.1 copy-start.8
  54.0 675.8 %reduce-scatter.3.cloned.1.call-start = ((), (), s32[]{:S(2)}) async-start(), calls=%async_computation.2 | async-start | bytes 270336 | tf_op jit(solution)/shard_map/reduce_scatter | solution.py:120
  54.7 443.3 %copy-start.9 = (f32[64,64]{1,0:T(8,128)}, f32[64,64]{1,0:T(8,128)S(1)}, u32[]{:S(2)}) copy-start(f32[64,64]{1,0:T(8,128)S(1)} %fusion.228) | copy-start | bytes 49156
  210.1 2.8 copy-start.2
  238.2 3.3 copy-start.6
  291.5 12.0 copy-start.7
  303.5 15.2 copy-start.10
  327.5 1.9 copy-start.5
  596.4 614.1 %reduce-scatter.5.cloned.1.call-start = ((), (), s32[]{:S(2)}) async-start(), calls=%async_computation.3 | async-start | bytes 270336 | tf_op jit(solution)/shard_map/reduce_scatter | solution.py:120
  804.2 1.9 copy-start.4
  1284.9 1.9 copy-start.3
  1537.0 5.7 copy-start.1
Sparse Core Ops, SparseCore 0:
  54.2 137.4 all-reduce.11
  596.5 133.2 reduce-scatter.2
  1077.6 132.8 reduce-scatter.4
where the time goes:
time: 1580 us; the launch traced here: 1550 us
  waiting for transfers between devices  403 us (26%)
  other arithmetic  392 us (25%)
  blocking collectives  249 us (16%)
  local copies, waits for them, and re-layouts  234 us (15%)
  between operations  155 us (10%)
  matrix products  115 us (7%)
    div x219, other arithmetic, lower_solve(): (target[column] - jnp.sum(factor[column] * result, axis=0)) / factor[colu...  267 us
    reduce_scatter x2, waiting for transfers between devices, per_device(): lax.psum_scatter(contract_rows(filled, ortho_rows), ('rows', 'sub'), scat...  266 us
    psum x1, waiting for transfers between devices, per_device(): gram_total, right_total = lax.psum((grams, right), ('rows', 'sub'))  137 us
    all_gather x2, blocking collectives, per_device(): mixer = lax.all_gather(mixer_share, ('rows', 'sub'), axis=0, tiled=True)  130 us
    psum x3, blocking collectives, per_device(): products = lax.psum(local_gram, ('rows', 'sub'))  119 us
    slice x192, local copies, waits for them, and re-layouts, cholesky_last(): diagonal_root = jnp.sqrt(remain[column])  113 us
    dot_general x3, matrix products, contract_rows(): lax.dot_general(former, latter, (((1,), (1,)), ((), ())), preferred_eleme...  42 us
    dot_general x4, matrix products, contract_first(): lax.dot_general(former, latter, (((0,), (0,)), ((), ())), preferred_eleme...  41.8 us
  transfers between devices with their start and end apart: 3, of which 3 were waited for; matrix products, arithmetic and copies ran while one was open for 0% of the time, Pallas kernels for 0%

commit v1 on v0

--- a/solution.py
+++ b/solution.py
@@ -7,6 +7,23 @@
 POWER = 2
 damping = 0.005
 highest = lax.Precision.HIGHEST
+
+
+def joined_along(blocks, dim):
+    blocks = jnp.moveaxis(blocks, 0, dim)
+    shape = blocks.shape
+    return blocks.reshape(*shape[:dim], shape[dim] * shape[dim + 1], *shape[dim + 2 :])
+
+
+def grow_blocks(shard, axis):
+    size, index = (lax.axis_size(axis), lax.axis_index(axis))
+    pieces, apart = (shard[None], 1)
+    while apart < size:
+        theirs = lax.ppermute(pieces, axis, [(i, i ^ apart) for i in range(size)])
+        low = index & apart == 0
+        pieces = jnp.concatenate([jnp.where(low, pieces, theirs), jnp.where(low, theirs, pieces)])
+        apart *= 2
+    return pieces
 
 
 def cholesky_last(system):
@@ -120,7 +137,7 @@
             mixer_share = lax.psum_scatter(
                 contract_rows(filled, ortho_rows), ("rows", "sub"), scatter_dimension=0, tiled=True
             ).astype(jnp.bfloat16)
-            mixer = lax.all_gather(mixer_share, ("rows", "sub"), axis=0, tiled=True)
+            mixer = joined_along(grow_blocks(mixer_share, ("rows", "sub")), 0)
     root_rows = math.sqrt(rows_all)
     new_basis = jnp.dot(inverse[:modes], sketch, precision=highest) * root_rows
     return (new_basis, coefficients)

time: 1580 us -> 1480 us (0.937)
  blocking collectives: 249 us -> 115 us
  waiting for transfers between devices: 403 us -> 438 us
    all_gather x2 -> x0, blocking collectives: 130 us -> none  [per_device(): mixer = lax.all_gather(mixer_share, ('rows', 'sub'), axis=0, tiled=True)]
    ppermute x0 -> x10, waiting for transfers between devices: none -> 33.8 us  [grow_blocks(): theirs = lax.ppermute(pieces, axis, [(i, i ^ apart) for i in range(size)])]
  transfers between devices with their start and end apart: 3 -> 13, of which waited for: 3 -> 13; matrix products, arithmetic and copies ran while one was open for 0% -> 0% of each run, Pallas kernels for 0% -> 0%
where the time goes in v1:
time: 1480 us; the launch traced here: 1450 us
  waiting for transfers between devices  438 us (30%)
  other arithmetic  394 us (27%)
  local copies, waits for them, and re-layouts  234 us (16%)
  between operations  155 us (10%)
  matrix products  116 us (8%)
  blocking collectives  115 us (8%)
    div x219, other arithmetic, lower_solve(): (target[column] - jnp.sum(factor[column] * result, axis=0)) / factor[colu...  267 us
    reduce_scatter x2, waiting for transfers between devices, per_device(): lax.psum_scatter(contract_rows(filled, ortho_rows), ('rows', 'sub'), scat...  267 us
    psum x1, waiting for transfers between devices, per_device(): gram_total, right_total = lax.psum((grams, right), ('rows', 'sub'))  137 us
    psum x3, blocking collectives, per_device(): products = lax.psum(local_gram, ('rows', 'sub'))  115 us
    slice x192, local copies, waits for them, and re-layouts, cholesky_last(): diagonal_root = jnp.sqrt(remain[column])  113 us
    dot_general x3, matrix products, contract_rows(): lax.dot_general(former, latter, (((1,), (1,)), ((), ())), preferred_eleme...  42.4 us
    dot_general x4, matrix products, contract_first(): lax.dot_general(former, latter, (((0,), (0,)), ((), ())), preferred_eleme...  41.8 us
    scatter x192, local copies, waits for them, and re-layouts, cholesky_last(): factor.at[:, column].set(jnp.where(lower_part, remain / diagonal_root, 0.0))  39.3 us
  transfers between devices with their start and end apart: 13, of which 13 were waited for; matrix products, arithmetic and copies ran while one was open for 0% of the time, Pallas kernels for 0%

profile of v1, /device:TPU:0, one launch (start us, length us, event | category | flops | bytes accessed | tf_op | source)
XLA Modules:
  0.0 1453.7 jit_solution(5655872848497916503)
XLA Ops:
  9.1 2.1 copy.518
  11.2 2.8 fusion.6
  14.1 2.5 copy.519
  16.6 12.6 mul.4313
  29.2 24.4 %fusion.2 = f32[32,512]{1,0:T(8,128)} fusion(bf16[32,16384]{1,0:T(8,128)(2,1)S(1)} %copy-done, bf16[512,16384]{1,0:T(8,128)(2,1)} %param.965, bf16[64,8,128,128]{3,2,1,0:T(8,128)(2,1)} %bitcast.3932), kind=kOutput, calls=%fused_computation.40 | convolution fusion | flops 545259520 | bytes 34668544 | tf_op jit(solution)/shard_map/dot_general | solution.py:95
  54.4 137.0 %all-reduce.12.cloned.1.call-done = (f32[32,32,512]{2,0,1:T(8,128)}, f32[32,512]{1,0:T(8,128)}) async-done(((f32[32,32,512]{2,0,1:T(8,128)}, f32[32,512]{1,0:T(8,128)}), (f32[32,32,512]{2,0,1:T(8,128)}, f32[32,512]{1,0:T(8,128)})) %all-reduce.12.cloned.1.call-update) | async-done | bytes 2162704 | tf_op jit(solution)/shard_map/psum | solution.py:117
  191.4 1.8 broadcast_add_fusion
  291.3 12.0 broadcast_in_dim.641
  303.2 15.2 %bitcast_select_fusion = bf16[512,16384]{1,0:T(8,128)(2,1)} fusion(bf16[512,16384]{1,0:T(8,128)(2,1)} %param.965, pred[64,8,128,128]{3,2,1,0:T(32,128)(4,1)} %bitcast.3933, bf16[32,16384]{1,0:T(8,128)(2,1)S(1)} %copy-done, f32[32,512]{1,0:T(8,128)S(1)} %scatter.1740), kind=kOutput, calls=%fused_computation | convolution fusion | flops 553664512 | bytes 43057152 | tf_op jit(solution)/shard_map/dot_general | solution.py:101
  318.4 8.8 fusion.224
  327.2 1.9 copy-done.5
  329.1 3.4 convolution_bitcast_fusion.2
  332.5 39.5 %psum.37 = f32[64,64,1]{1,0,2:T(8,128)S(1)} all-reduce(f32[64,64,1]{1,0,2:T(8,128)S(1)} %convolution_bitcast_fusion.2), channel_id=1, replica_groups=mesh['rows'=8,'sub'=4] {'rows','sub'}, use_global_device_ids=true, to_apply=%region_97.98 | all-reduce | flops 4096 | bytes 32768 | tf_op jit(solution)/shard_map/psum | solution.py:133
  499.9 1.4 fusion.504
  509.9 1.4 fusion.497
  515.7 1.4 fusion.493
  530.0 1.4 fusion.483
  565.7 1.4 fusion.458
  578.4 1.4 fusion.449
  581.3 6.0 convolution_convert_fusion.2
  587.2 8.8 fusion.526
  596.5 133.1 %reduce-scatter.3.cloned.1.call-done = f32[16,64]{1,0:T(8,128)} async-done(((f32[512,64]{1,0:T(8,128)}), f32[16,64]{1,0:T(8,128)}) %reduce-scatter.3.cloned.1.call-update) | async-done | bytes 4112 | tf_op jit(solution)/shard_map/reduce_scatter | solution.py:137
  730.3 3.6 collective-permute-done
  734.7 4.5 collective-permute-done.1
  740.6 3.9 collective-permute-done.3
  745.1 3.7 collective-permute-done.4
  748.9 8.9 fusion.527
  757.9 1.9 copy-done.4
  759.8 3.4 convolution_bitcast_fusion.1
  763.2 37.9 %psum.38 = f32[64,64,1]{1,0,2:T(8,128)S(1)} all-reduce(f32[64,64,1]{1,0,2:T(8,128)S(1)} %convolution_bitcast_fusion.1), channel_id=1, replica_groups=mesh['rows'=8,'sub'=4] {'rows','sub'}, use_global_device_ids=true, to_apply=%region_226.227 | all-reduce | flops 4096 | bytes 32768 | tf_op jit(solution)/shard_map/psum | solution.py:133
  922.0 1.9 subtract_divide_fusion.3
  924.0 1.4 fusion.447
  925.5 1.4 fusion.446
  931.2 1.4 fusion.442
  932.7 1.4 fusion.441
  942.7 1.4 fusion.434
  948.5 1.4 fusion.430
  962.8 1.4 fusion.420
  998.5 1.4 fusion.395
  1011.2 1.4 fusion.386
  1014.1 6.0 convolution_convert_fusion.1
  1020.1 9.2 fusion.528
  1029.3 133.6 %reduce-scatter.5.cloned.1.call-done = f32[16,64]{1,0:T(8,128)} async-done(((f32[512,64]{1,0:T(8,128)}), f32[16,64]{1,0:T(8,128)}) %reduce-scatter.5.cloned.1.call-update) | async-done | bytes 4112 | tf_op jit(solution)/shard_map/reduce_scatter | solution.py:137
  1163.6 3.6 collective-permute-done.5
  1167.9 4.5 collective-permute-done.6
  1173.9 3.9 collective-permute-done.8
  1178.4 3.7 collective-permute-done.9
  1182.2 8.9 fusion.529
  1191.1 1.9 copy-done.3
  1193.1 3.4 convolution_bitcast_fusion
  1196.5 37.9 %psum.39 = f32[64,64,1]{1,0,2:T(8,128)S(1)} all-reduce(f32[64,64,1]{1,0,2:T(8,128)S(1)} %convolution_bitcast_fusion), channel_id=1, replica_groups=mesh['rows'=8,'sub'=4] {'rows','sub'}, use_global_device_ids=true, to_apply=%region_355.356 | all-reduce | flops 4096 | bytes 32768 | tf_op jit(solution)/shard_map/psum | solution.py:133
  1354.7 1.9 subtract_divide_fusion.2
  1356.7 1.4 fusion.384
  1359.6 1.4 fusion.382
  1366.9 1.4 fusion.377
  1371.1 1.4 fusion.374
  1372.6 1.4 fusion.373
  1386.9 1.4 fusion.363
  1402.6 1.4 fusion.352
  1412.7 1.4 fusion.345
  1424.2 1.4 fusion.337
  1434.2 1.4 fusion.330
  1437.0 1.4 fusion.328
  1441.2 5.7 convolution_multiply_fusion
  (2340 shorter events, 557.1 us)
Async XLA Ops:
  7.2 1.3 copy-start
  7.2 184.2 %all-reduce.12.cloned.1.call-start = ((), (), s32[]{:S(2)}) async-start(), calls=%async_computation.4 | async-start | bytes 4325376 | tf_op jit(solution)/shard_map/psum | solution.py:117
  9.1 2.1 copy-start.8
  53.7 675.9 %reduce-scatter.3.cloned.1.call-start = ((), (), s32[]{:S(2)}) async-start(), calls=%async_computation.2 | async-start | bytes 270336 | tf_op jit(solution)/shard_map/reduce_scatter | solution.py:137
  54.4 443.3 %copy-start.9 = (f32[64,64]{1,0:T(8,128)}, f32[64,64]{1,0:T(8,128)S(1)}, u32[]{:S(2)}) copy-start(f32[64,64]{1,0:T(8,128)S(1)} %fusion.228) | copy-start | bytes 49156
  210.1 2.8 copy-start.2
  238.2 3.3 copy-start.6
  291.2 12.0 copy-start.7
  303.2 15.2 %copy-start.10 = (s32[512,64]{0,1:T(8,128)S(1)}, s32[512,64]{0,1:T(8,128)}, u32[]{:S(2)}) copy-start(s32[512,64]{0,1:T(8,128)} %param.967) | copy-start | bytes 393220
  327.2 1.9 copy-start.5
  596.1 566.8 %reduce-scatter.5.cloned.1.call-start = ((), (), s32[]{:S(2)}) async-start(), calls=%async_computation.3 | async-start | bytes 270336 | tf_op jit(solution)/shard_map/reduce_scatter | solution.py:137
  730.3 3.6 collective-permute-start
  734.6 4.6 collective-permute-start.1
  739.2 1.2 collective-permute-start.2
  740.5 4.0 collective-permute-start.3
  744.5 4.3 collective-permute-start.4
  757.8 1.9 copy-start.4
  1163.5 3.6 collective-permute-start.5
  1167.9 4.6 collective-permute-start.6
  1172.5 1.2 collective-permute-start.7
  1173.8 4.0 collective-permute-start.8
  1177.8 4.3 collective-permute-start.9
  1191.1 1.9 copy-start.3
  1441.2 5.7 copy-start.1
Sparse Core Ops, SparseCore 0:
  53.8 137.5 all-reduce.11
  596.2 133.3 reduce-scatter.2
  1029.4 133.3 reduce-scatter.4
